TPU v7x, 32 devices: a whole 2x2x4 slice. The times are simulated.
32 devices in a mesh: expert: 4 (over y, core), dp: 8 (over z, x).
Axes of the slice: x: 2, y: 2, z: 4, core: 2. Of those that a mesh axis runs over, the one named last changes fastest.
Arguments:
- tokens: bfloat16 [2048, 3584], P(('dp', 'expert')), parts along dimension 0, may hold values from -6 to 6
- expert_ids: int32 [2048, 1], P(('dp', 'expert')), parts along dimension 0, may hold values from 0 to 3; in each aligned block of 64 rows (0 to 63, 64 to 127, ...) at most 18 rows name the same one
- combine: bfloat16 [2048, 1], P(('dp', 'expert')), parts along dimension 0, may hold values from 0.19921875 to 1
- w_gate: bfloat16 [3584, 8192], P(None, 'expert'), may hold values from -0.09375 to 0.09375
- w_up: bfloat16 [3584, 8192], P(None, 'expert'), may hold values from -0.09375 to 0.09375
- w_down: bfloat16 [8192, 3584], P('expert'), may hold values from -0.125 to 0.125
Outputs:
- mixed: bfloat16 [2048, 3584], P(('dp', 'expert')), parts along dimension 0
There are 8 independent parts, one for each index of `dp`. A program takes and returns all parts, laid end to end along the dimension named above; an argument that names none is the same for every part. Nothing has to cross between parts.
Inputs may be any that keep to these rules, and one draw needn't show every extreme that they name: `expert_ids`: each token names one expert. Among the 64 tokens of one device (aligned blocks of rows) no expert is named more than 18 times, a bound that some block reaches.
All inputs are finite; a program needn't handle non-finite values.
Results may differ from a plain program's by a relative error of at most 0.0057.
Values may be sent and summed in bfloat16 or wider, within the bound.
A program may use at most 128 MiB of HBM per device.

v0:
```python
import jax
import jax.numpy as jnp
from jax import lax
from jax.sharding import PartitionSpec as P

EXPERTS = 4
TOP = 1
CAP = 18


def local(tokens, expert_ids, combine, w_gate, w_up, w_down):
    devices = lax.axis_size("expert")
    span_size = devices // EXPERTS
    model_width = tokens.shape[1]
    token_count = tokens.shape[0]
    flat_ids = expert_ids.reshape(-1)
    labels = jnp.arange(EXPERTS, dtype=jnp.int32)
    member = (flat_ids[:, None] == labels[None, :]).astype(jnp.int32)
    rank_table = jnp.cumsum(member, axis=0) - 1
    positions = jnp.sum(member * rank_table, axis=1)
    slot_ids = jnp.arange(CAP, dtype=jnp.int32)
    placed = (member.T[:, None, :] == 1) & (positions[None, None, :] == slot_ids[None, :, None])
    repeated = jnp.repeat(tokens, TOP, axis=0)
    outgoing = jnp.einsum(
        "ecf,fd->ecd", placed.astype(jnp.bfloat16), repeated, preferred_element_type=jnp.float32
    ).astype(jnp.bfloat16)
    outgoing = jnp.repeat(outgoing, span_size, axis=0)
    arrived = lax.all_to_all(outgoing, "expert", split_axis=0, concat_axis=0, tiled=True)
    slot_count = arrived.shape[1]
    row_block = arrived.reshape(-1, model_width)
    gate_values = jnp.dot(row_block, w_gate, preferred_element_type=jnp.float32)
    up_values = jnp.dot(row_block, w_up, preferred_element_type=jnp.float32)
    hidden = (jax.nn.silu(gate_values) * up_values).astype(jnp.bfloat16)
    result = (
        jnp.dot(hidden, w_down, preferred_element_type=jnp.float32)
        .astype(jnp.bfloat16)
        .reshape(devices, slot_count, model_width)
    )
    returned_rows = lax.all_to_all(result, "expert", split_axis=0, concat_axis=0, tiled=True)
    summed = jnp.sum(
        returned_rows.astype(jnp.float32).reshape(EXPERTS, span_size, CAP, model_width), axis=1
    )
    weighted = placed.astype(jnp.float32) * combine.astype(jnp.float32).reshape(-1)[None, None, :]
    entry_rows = jnp.einsum("ecf,ecd->fd", weighted, summed, precision=lax.Precision.HIGHEST)
    mixed_rows = jnp.sum(entry_rows.reshape(token_count, TOP, model_width), axis=1)
    return mixed_rows.astype(jnp.bfloat16)


def solution(mesh):
    placed = (
        P(("dp", "expert"), None),
        P(("dp", "expert"), None),
        P(("dp", "expert"), None),
        P(None, "expert"),
        P(None, "expert"),
        P("expert", None),
    )
    return jax.shard_map(
        local, mesh=mesh, in_specs=placed, out_specs=P(("dp", "expert"), None), check_vma=False
    )
```

profile of v0, /device:TPU:0, one launch (start us, length us, event | category | flops | bytes accessed | tf_op | source)
XLA Modules:
  0.0 56.4 jit_solution(2965514269756863854)
XLA Ops:
  0.0 0.0 copy-start
  0.0 0.8 %fusion.5 = s32[64,4]{1,0:T(8,128)S(1)} fusion(s32[64]{0:T(128)} %bitcast.17), kind=kLoop, calls=%fused_computation.12 | loop fusion | flops 512 | bytes 1280 | tf_op jit(solution)/shard_map/convert_element_type | solution.py:18
  0.8 0.7 %convert_compare_fusion = pred[4,64]{1,0:T(4,128)(4,1)S(1)} fusion(s32[64]{0:T(128)} %bitcast.18), kind=kLoop, calls=%fused_computation.20 | loop fusion | flops 768 | bytes 512 | tf_op jit(solution)/shard_map/eq | solution.py:22
  1.4 0.1 reduce_window_sum.11
  1.5 0.8 %select_reduce_fusion = s32[64]{0:T(128)S(1)} fusion(s32[64,4]{1,0:T(8,128)S(1)} %reduce_window_sum.11, s32[64]{0:T(128)} %bitcast.19), kind=kLoop, calls=%fused_computation.10 | loop fusion | flops 960 | bytes 1536 | tf_op jit(solution)/shard_map/reduce_sum | solution.py:20
  2.4 0.0 copy-done
  2.4 0.3 convolution_convert_fusion
  2.7 14.6 %all_to_all.10 = bf16[4,18,3584]{2,1,0:T(8,128)(2,1)S(1)} all-to-all(bf16[4,18,3584]{2,1,0:T(8,128)(2,1)S(1)} %convolution_convert_fusion), channel_id=1, replica_groups=mesh['expert'=4,'dp'=8] {'expert'}, dimensions={0} | all-to-all | bytes 1032192 | tf_op jit(solution)/shard_map/all_to_all | solution.py:28
  17.4 0.2 reshape.60
  17.5 7.8 %fusion.14 = f32[72,2048]{1,0:T(8,128)S(1)} fusion(bf16[72,3584]{1,0:T(8,128)(2,1)S(1)} %reshape.60, bf16[3584,2048]{1,0:T(8,128)(2,1)} %param.9), kind=kOutput, calls=%fused_computation.25 | convolution fusion | flops 1056964608 | bytes 15785984 | tf_op jit(solution)/shard_map/dot_general | solution.py:31
  25.4 0.0 copy-start.1
  25.4 14.6 %convolution_convert_fusion.1 = bf16[72,3584]{1,0:T(8,128)(2,1)S(1)} fusion(bf16[2048,3584]{1,0:T(8,128)(2,1)} %param.11, bf16[72,3584]{1,0:T(8,128)(2,1)S(1)} %reshape.60, bf16[3584,2048]{1,0:T(8,128)(2,1)} %param.10, f32[72,2048]{1,0:T(8,128)S(1)} %fusion.14), kind=kOutput, calls=%fused_computation.2 | convolution fusion | flops 2115072000 | bytes 30982144 | tf_op jit(solution)/shard_map/dot_general | solution.py:35
  40.0 1.0 %reshape.61 = bf16[4,18,3584]{2,1,0:T(8,128)(2,1)} reshape(bf16[72,3584]{1,0:T(8,128)(2,1)S(1)} %convolution_convert_fusion.1) | data formatting | bytes 1032192 | tf_op jit(solution)/shard_map/reshape | solution.py:37
  41.0 3.5 %all-to-all-start.1 = ((bf16[4,18,3584]{2,1,0:T(8,128)(2,1)}), bf16[4,18,3584]{2,1,0:T(8,128)(2,1)S(1)}, u32[]{:S(2)}, u32[]{:S(2)}) async-start(bf16[4,18,3584]{2,1,0:T(8,128)(2,1)} %reshape.61), calls=%async_computation.1 | async-start | bytes 1376256 | tf_op jit(solution)/shard_map/all_to_all | solution.py:39
  44.5 0.0 copy-done.1
  44.5 10.5 %all-to-all-done.1 = bf16[4,18,3584]{2,1,0:T(8,128)(2,1)S(1)} async-done(((bf16[4,18,3584]{2,1,0:T(8,128)(2,1)}), bf16[4,18,3584]{2,1,0:T(8,128)(2,1)S(1)}, u32[]{:S(2)}, u32[]{:S(2)}) %all-to-all-start.1) | async-done | bytes 516128 | tf_op jit(solution)/shard_map/all_to_all | solution.py:39
  55.0 1.4 %fusion = bf16[64,3584]{1,0:T(8,128)(2,1)} fusion(bf16[4,18,3584]{2,1,0:T(8,128)(2,1)S(1)} %all-to-all-done.1, f32[64]{0:T(128)S(1)} %bitcast_convert_fusion, pred[18,64]{1,0:T(8,128)(4,1)S(1)} %iota_compare_fusion.1, pred[4,64]{1,0:T(4,128)(4,1)S(1)} %convert_compare_fusion), kind=kOutput, calls=%fused_computation.3 | convolution fusion | flops 198419456 | bytes 976512 | tf_op jit(solution)/shard_map/ecf,ecd->fd/dot_general | solution.py:44
  (2 shorter events, 0.0 us)
Async XLA Ops:
  0.0 2.4 %copy-start = (bf16[64,3584]{1,0:T(8,128)(2,1)S(1)}, bf16[64,3584]{1,0:T(8,128)(2,1)}, u32[]{:S(2)}) copy-start(bf16[64,3584]{1,0:T(8,128)(2,1)} %param.6) | copy-start | bytes 1376260
  25.4 19.1 %copy-start.1 = (bf16[64,1]{0,1:T(2,128)(2,1)S(1)}, bf16[64,1]{0,1:T(2,128)(2,1)}, u32[]{:S(2)}) copy-start(bf16[64,1]{0,1:T(2,128)(2,1)} %param.8) | copy-start | bytes 388
  41.0 14.0 %all-to-all-start.1 = ((bf16[4,18,3584]{2,1,0:T(8,128)(2,1)}), bf16[4,18,3584]{2,1,0:T(8,128)(2,1)S(1)}, u32[]{:S(2)}, u32[]{:S(2)}) async-start(bf16[4,18,3584]{2,1,0:T(8,128)(2,1)} %reshape.61), calls=%async_computation.1 | async-start | bytes 1376256 | tf_op jit(solution)/shard_map/all_to_all | solution.py:39
where the time goes:
time: 56.7 us; the launch traced here: 56.4 us
  matrix products  24.1 us (43%)
  blocking collectives  14.6 us (26%)
  waiting for transfers between devices  10.5 us (19%)
  starting transfers between devices  3.48 us (6%)
  other arithmetic  2.38 us (4%)
  local copies, waits for them, and re-layouts  1.19 us (2%)
    all_to_all x1, blocking collectives, local(): lax.all_to_all(outgoing, 'expert', split_axis=0, concat_axis=0, tiled=True)  14.6 us
    dot_general x1, matrix products, local(): jnp.dot(hidden, w_down, preferred_element_type=jnp.float32)  14.6 us
    all_to_all x1, waiting for transfers between devices, local(): lax.all_to_all(result, 'expert', split_axis=0, concat_axis=0, tiled=True)  10.5 us
    dot_general x1, matrix products, local(): gate_values = jnp.dot(row_block, w_gate, preferred_element_type=jnp.float32)  7.85 us
    all_to_all x1, starting transfers between devices, local(): lax.all_to_all(result, 'expert', split_axis=0, concat_axis=0, tiled=True)  3.48 us
    dot_general x1, matrix products, local(): jnp.einsum('ecf,ecd->fd', weighted, summed, precision=lax.Precision.HIGHEST)  1.35 us
  transfers between devices with their start and end apart: 1, of which 1 were waited for; matrix products, arithmetic and copies ran while one was open for 0% of the time, Pallas kernels for 0%

commit v1 on v0

--- a/solution.py
+++ b/solution.py
@@ -6,6 +6,29 @@
 EXPERTS = 4
 TOP = 1
 CAP = 18
+
+
+def in_blocks(shard, dim, count):
+    shape = shard.shape
+    parts = shard.reshape(*shape[:dim], count, shape[dim] // count, *shape[dim + 1 :])
+    return jnp.moveaxis(parts, dim, 0)
+
+
+def in_order(blocks, dim):
+    lengths = list(blocks.shape[1:])
+    lengths[dim] *= blocks.shape[0]
+    return jnp.moveaxis(blocks, 0, dim).reshape(lengths)
+
+
+def sent_to_each(value, axis, split_dim, concat_dim):
+    length, index = (lax.axis_size(axis), lax.axis_index(axis))
+    blocks = in_blocks(value, split_dim, length)
+    outs = [blocks[index]]
+    for step in range(1, length):
+        sent = blocks[(index + step) % length]
+        outs.append(lax.ppermute(sent, axis, [(i, (i + step) % length) for i in range(length)]))
+    blocks = jnp.stack(outs)[(index - jnp.arange(length)) % length]
+    return in_order(blocks, concat_dim)
 
 
 def local(tokens, expert_ids, combine, w_gate, w_up, w_down):
@@ -25,7 +48,7 @@
         "ecf,fd->ecd", placed.astype(jnp.bfloat16), repeated, preferred_element_type=jnp.float32
     ).astype(jnp.bfloat16)
     outgoing = jnp.repeat(outgoing, span_size, axis=0)
-    arrived = lax.all_to_all(outgoing, "expert", split_axis=0, concat_axis=0, tiled=True)
+    arrived = sent_to_each(outgoing, "expert", 0, 0)
     slot_count = arrived.shape[1]
     row_block = arrived.reshape(-1, model_width)
     gate_values = jnp.dot(row_block, w_gate, preferred_element_type=jnp.float32)

time: 56.7 us -> 53.9 us (0.951)
  blocking collectives: 14.6 us -> 0 us
  waiting for transfers between devices: 10.5 us -> 17.1 us
  starting transfers between devices: 3.48 us -> 7.99 us
  local copies, waits for them, and re-layouts: 1.19 us -> 1.87 us
    all_to_all x1 -> x0, blocking collectives: 14.6 us -> none  [local(): lax.all_to_all(outgoing, 'expert', split_axis=0, concat_axis=0, tiled=True)]
    ppermute x0 -> x3, waiting for transfers between devices: none -> 6.39 us  [sent_to_each(): lax.ppermute(sent, axis, [(i, (i + step) % length) for i in range(length)])]
    ppermute x0 -> x3, starting transfers between devices: none -> 4.51 us  [sent_to_each(): lax.ppermute(sent, axis, [(i, (i + step) % length) for i in range(length)])]
    gather x0 -> x1, local copies, waits for them, and re-layouts: none -> 0.59 us  [sent_to_each(): blocks = jnp.stack(outs)[(index - jnp.arange(length)) % length]]
  transfers between devices with their start and end apart: 1 -> 4, of which waited for: 1 -> 4; matrix products, arithmetic and copies ran while one was open for 0% -> 0% of each run, Pallas kernels for 0% -> 0%
where the time goes in v1:
time: 53.9 us; the launch traced here: 53.7 us
  matrix products  24.1 us (45%)
  waiting for transfers between devices  17.1 us (32%)
  starting transfers between devices  7.99 us (15%)
  other arithmetic  2.51 us (5%)
  local copies, waits for them, and re-layouts  1.87 us (3%)
    dot_general x1, matrix products, local(): jnp.dot(hidden, w_down, preferred_element_type=jnp.float32)  14.6 us
    all_to_all x1, waiting for transfers between devices, local(): lax.all_to_all(result, 'expert', split_axis=0, concat_axis=0, tiled=True)  10.7 us
    dot_general x1, matrix products, local(): gate_values = jnp.dot(row_block, w_gate, preferred_element_type=jnp.float32)  7.85 us
    ppermute x3, waiting for transfers between devices, sent_to_each(): lax.ppermute(sent, axis, [(i, (i + step) % length) for i in range(length)])  6.39 us
    ppermute x3, starting transfers between devices, sent_to_each(): lax.ppermute(sent, axis, [(i, (i + step) % length) for i in range(length)])  4.51 us
    all_to_all x1, starting transfers between devices, local(): lax.all_to_all(result, 'expert', split_axis=0, concat_axis=0, tiled=True)  3.48 us
    dot_general x1, matrix products, local(): jnp.einsum('ecf,ecd->fd', weighted, summed, precision=lax.Precision.HIGHEST)  1.35 us
  transfers between devices with their start and end apart: 4, of which 4 were waited for; matrix products, arithmetic and copies ran while one was open for 0% of the time, Pallas kernels for 0%

profile of v1, /device:TPU:0, one launch (start us, length us, event | category | flops | bytes accessed | tf_op | source)
XLA Modules:
  0.0 53.7 jit_solution(1783439300907811036)
XLA Ops:
  0.0 0.0 copy-start
  0.0 0.8 %fusion.5 = s32[64,4]{1,0:T(8,128)S(1)} fusion(s32[64]{0:T(128)} %bitcast.29), kind=kLoop, calls=%fused_computation.15 | loop fusion | flops 512 | bytes 1280 | tf_op jit(solution)/shard_map/convert_element_type | solution.py:41
  0.8 0.7 %convert_compare_fusion = pred[4,64]{1,0:T(4,128)(4,1)S(1)} fusion(s32[64]{0:T(128)} %bitcast.30), kind=kLoop, calls=%fused_computation.27 | loop fusion | flops 768 | bytes 512 | tf_op jit(solution)/shard_map/eq | solution.py:45
  1.4 0.1 reduce_window_sum.11
  1.5 0.8 %select_reduce_fusion = s32[64]{0:T(128)S(1)} fusion(s32[64,4]{1,0:T(8,128)S(1)} %reduce_window_sum.11, s32[64]{0:T(128)} %bitcast.31), kind=kLoop, calls=%fused_computation.13 | loop fusion | flops 960 | bytes 1536 | tf_op jit(solution)/shard_map/reduce_sum | solution.py:43
  2.4 0.0 copy-done
  2.4 0.3 convolution_convert_fusion
  2.7 0.1 dynamic-slice_bitcast_fusion
  2.8 0.5 %collective-permute-start = (bf16[1,18,3584]{2,1,0:T(8,128)(2,1)S(1)}, bf16[1,18,3584]{2,1,0:T(8,128)(2,1)S(1)}, u32[]{:S(2)}, u32[]{:S(2)}) collective-permute-start(bf16[1,18,3584]{2,1,0:T(8,128)(2,1)S(1)} %get-tuple-element.8), channel_id=1, source_target_pairs={{0,8},{8,16},{16,24},{24,0},{1,9},{9,17},{17,25},{25,1},{2,10},{10... | collective-permute-start | bytes 387080 | tf_op jit(solution)/shard_map/ppermute | solution.py:29
  3.4 2.6 %collective-permute-start.1 = (bf16[1,18,3584]{2,1,0:T(8,128)(2,1)S(1)}, bf16[1,18,3584]{2,1,0:T(8,128)(2,1)S(1)}, u32[]{:S(2)}, u32[]{:S(2)}) collective-permute-start(bf16[1,18,3584]{2,1,0:T(8,128)(2,1)S(1)} %get-tuple-element.7), channel_id=1, source_target_pairs={{0,16},{8,24},{16,0},{24,8},{1,17},{9,25},{17,1},{25,9},{2,18},{10... | collective-permute-start | bytes 387080 | tf_op jit(solution)/shard_map/ppermute | solution.py:29
  5.9 1.4 %collective-permute-start.2 = (bf16[1,18,3584]{2,1,0:T(8,128)(2,1)S(1)}, bf16[1,18,3584]{2,1,0:T(8,128)(2,1)S(1)}, u32[]{:S(2)}, u32[]{:S(2)}) collective-permute-start(bf16[1,18,3584]{2,1,0:T(8,128)(2,1)S(1)} %get-tuple-element.6), channel_id=1, source_target_pairs={{0,24},{8,0},{16,8},{24,16},{1,25},{9,1},{17,9},{25,17},{2,26},{10... | collective-permute-start | bytes 387080 | tf_op jit(solution)/shard_map/ppermute | solution.py:29
  7.4 1.9 %collective-permute-done = bf16[1,18,3584]{2,1,0:T(8,128)(2,1)S(1)} collective-permute-done((bf16[1,18,3584]{2,1,0:T(8,128)(2,1)S(1)}, bf16[1,18,3584]{2,1,0:T(8,128)(2,1)S(1)}, u32[]{:S(2)}, u32[]{:S(2)}) %collective-permute-start) | collective-permute-done | bytes 129056 | tf_op jit(solution)/shard_map/ppermute | solution.py:29
  9.3 1.9 %collective-permute-done.1 = bf16[1,18,3584]{2,1,0:T(8,128)(2,1)S(1)} collective-permute-done((bf16[1,18,3584]{2,1,0:T(8,128)(2,1)S(1)}, bf16[1,18,3584]{2,1,0:T(8,128)(2,1)S(1)}, u32[]{:S(2)}, u32[]{:S(2)}) %collective-permute-start.1) | collective-permute-done | bytes 129056 | tf_op jit(solution)/shard_map/ppermute | solution.py:29
  11.2 2.6 %collective-permute-done.2 = bf16[1,18,3584]{2,1,0:T(8,128)(2,1)S(1)} collective-permute-done((bf16[1,18,3584]{2,1,0:T(8,128)(2,1)S(1)}, bf16[1,18,3584]{2,1,0:T(8,128)(2,1)S(1)}, u32[]{:S(2)}, u32[]{:S(2)}) %collective-permute-start.2) | collective-permute-done | bytes 129056 | tf_op jit(solution)/shard_map/ppermute | solution.py:29
  13.7 0.1 maximum_bitcast_fusion
  13.9 0.6 %gather_fusion = bf16[4,18,3584]{2,1,0:T(8,128)(2,1)S(1)} fusion(bf16[4,18,3584]{2,1,0:T(8,128)(2,1)S(1)} %maximum_bitcast_fusion, s32[1024]{0:T(1024)S(1)} %pad_clamp_fusion), kind=kCustom, calls=%fused_computation | custom fusion | bytes 1032208 | tf_op jit(solution)/shard_map/gather | solution.py:30
  14.5 0.2 reshape_reshape.3
  14.6 7.8 %fusion.16 = f32[72,2048]{1,0:T(8,128)S(1)} fusion(bf16[72,3584]{1,0:T(8,128)(2,1)S(1)} %reshape_reshape.3, bf16[3584,2048]{1,0:T(8,128)(2,1)} %param.9), kind=kOutput, calls=%fused_computation.38 | convolution fusion | flops 1056964608 | bytes 15785984 | tf_op jit(solution)/shard_map/dot_general | solution.py:54
  22.5 0.0 copy-start.1
  22.5 14.6 %convolution_convert_fusion.1 = bf16[72,3584]{1,0:T(8,128)(2,1)S(1)} fusion(bf16[2048,3584]{1,0:T(8,128)(2,1)} %param.11, bf16[72,3584]{1,0:T(8,128)(2,1)S(1)} %reshape_reshape.3, bf16[3584,2048]{1,0:T(8,128)(2,1)} %param.10, f32[72,2048]{1,0:T(8,128)S(1)} %fusion.16), kind=kOutput, calls=%fused_computation.3 | convolution fusion | flops 2115072000 | bytes 30982144 | tf_op jit(solution)/shard_map/dot_general | solution.py:58
  37.1 1.0 %reshape.113 = bf16[4,18,3584]{2,1,0:T(8,128)(2,1)} reshape(bf16[72,3584]{1,0:T(8,128)(2,1)S(1)} %convolution_convert_fusion.1) | data formatting | bytes 1032192 | tf_op jit(solution)/shard_map/reshape | solution.py:60
  38.1 3.5 %all-to-all-start = ((bf16[4,18,3584]{2,1,0:T(8,128)(2,1)}), bf16[4,18,3584]{2,1,0:T(8,128)(2,1)S(1)}, u32[]{:S(2)}, u32[]{:S(2)}) async-start(bf16[4,18,3584]{2,1,0:T(8,128)(2,1)} %reshape.113), calls=%async_computation | async-start | bytes 1376256 | tf_op jit(solution)/shard_map/all_to_all | solution.py:62
  41.6 0.0 copy-done.1
  41.6 10.7 %all-to-all-done = bf16[4,18,3584]{2,1,0:T(8,128)(2,1)S(1)} async-done(((bf16[4,18,3584]{2,1,0:T(8,128)(2,1)}), bf16[4,18,3584]{2,1,0:T(8,128)(2,1)S(1)}, u32[]{:S(2)}, u32[]{:S(2)}) %all-to-all-start) | async-done | bytes 516128 | tf_op jit(solution)/shard_map/all_to_all | solution.py:62
  52.3 1.4 %fusion = bf16[64,3584]{1,0:T(8,128)(2,1)} fusion(bf16[4,18,3584]{2,1,0:T(8,128)(2,1)S(1)} %all-to-all-done, f32[64]{0:T(128)S(1)} %bitcast_convert_fusion, pred[18,64]{1,0:T(8,128)(4,1)S(1)} %iota_compare_fusion.1, pred[4,64]{1,0:T(4,128)(4,1)S(1)} %convert_compare_fusion), kind=kOutput, calls=%fused_computation.4 | convolution fusion | flops 198419456 | bytes 976512 | tf_op jit(solution)/shard_map/ecf,ecd->fd/dot_general | solution.py:67
  (4 shorter events, 0.0 us)
Async XLA Ops:
  0.0 2.4 %copy-start = (bf16[64,3584]{1,0:T(8,128)(2,1)S(1)}, bf16[64,3584]{1,0:T(8,128)(2,1)}, u32[]{:S(2)}) copy-start(bf16[64,3584]{1,0:T(8,128)(2,1)} %param.6) | copy-start | bytes 1376260
  2.8 6.5 %collective-permute-start = (bf16[1,18,3584]{2,1,0:T(8,128)(2,1)S(1)}, bf16[1,18,3584]{2,1,0:T(8,128)(2,1)S(1)}, u32[]{:S(2)}, u32[]{:S(2)}) collective-permute-start(bf16[1,18,3584]{2,1,0:T(8,128)(2,1)S(1)} %get-tuple-element.8), channel_id=1, source_target_pairs={{0,8},{8,16},{16,24},{24,0},{1,9},{9,17},{17,25},{25,1},{2,10},{10... | collective-permute-start | bytes 387080 | tf_op jit(solution)/shard_map/ppermute | solution.py:29
  3.4 7.8 %collective-permute-start.1 = (bf16[1,18,3584]{2,1,0:T(8,128)(2,1)S(1)}, bf16[1,18,3584]{2,1,0:T(8,128)(2,1)S(1)}, u32[]{:S(2)}, u32[]{:S(2)}) collective-permute-start(bf16[1,18,3584]{2,1,0:T(8,128)(2,1)S(1)} %get-tuple-element.7), channel_id=1, source_target_pairs={{0,16},{8,24},{16,0},{24,8},{1,17},{9,25},{17,1},{25,9},{2,18},{10... | collective-permute-start | bytes 387080 | tf_op jit(solution)/shard_map/ppermute | solution.py:29
  5.9 7.8 %collective-permute-start.2 = (bf16[1,18,3584]{2,1,0:T(8,128)(2,1)S(1)}, bf16[1,18,3584]{2,1,0:T(8,128)(2,1)S(1)}, u32[]{:S(2)}, u32[]{:S(2)}) collective-permute-start(bf16[1,18,3584]{2,1,0:T(8,128)(2,1)S(1)} %get-tuple-element.6), channel_id=1, source_target_pairs={{0,24},{8,0},{16,8},{24,16},{1,25},{9,1},{17,9},{25,17},{2,26},{10... | collective-permute-start | bytes 387080 | tf_op jit(solution)/shard_map/ppermute | solution.py:29
  22.5 19.1 %copy-start.1 = (bf16[64,1]{0,1:T(2,128)(2,1)S(1)}, bf16[64,1]{0,1:T(2,128)(2,1)}, u32[]{:S(2)}) copy-start(bf16[64,1]{0,1:T(2,128)(2,1)} %param.8) | copy-start | bytes 388
  38.1 14.2 %all-to-all-start = ((bf16[4,18,3584]{2,1,0:T(8,128)(2,1)}), bf16[4,18,3584]{2,1,0:T(8,128)(2,1)S(1)}, u32[]{:S(2)}, u32[]{:S(2)}) async-start(bf16[4,18,3584]{2,1,0:T(8,128)(2,1)} %reshape.113), calls=%async_computation | async-start | bytes 1376256 | tf_op jit(solution)/shard_map/all_to_all | solution.py:62
